TPU v7x, 512 devices: a whole 4x4x16 slice. The times are simulated.
512 devices in a mesh: dp: 16 (over x, y_hi, core), ctx: 32 (over y_lo, z).
Axes of the slice: x: 4, y: 4 (y_hi: 2, y_lo: 2; y = y_hi * 2 + y_lo), z: 16, core: 2. Of those that a mesh axis runs over, the one named last changes fastest.
Arguments:
- queries: bfloat16 [16, 4096, 2048], P('dp', 'ctx'), may hold values from -6 to 6
- keys: bfloat16 [16, 4096, 2048], P('dp', 'ctx'), may hold values from -6 to 6
- values: bfloat16 [16, 4096, 2048], P('dp', 'ctx'), may hold values from -6 to 6
- out_grad: bfloat16 [16, 4096, 2048], P('dp', 'ctx'), may hold values from -6 to 6
- out_proj: bfloat16 [2048, 2048], P('dp'), may hold values from -0.125 to 0.125
- attn_out: bfloat16 [16, 4096, 2048], P('dp', 'ctx'), may hold values from -3 to 3
- log_sum: float32 [16, 16, 4096], P('dp', None, 'ctx'), may hold values from 3 to 5
- group_order: int32 [16, 128], P('dp'), may hold values from 0 to 127, each once within a row
Outputs:
- query_grad: bfloat16 [16, 4096, 2048], P('dp', 'ctx')
- key_grad: bfloat16 [16, 4096, 2048], P('dp', 'ctx')
- value_grad: bfloat16 [16, 4096, 2048], P('dp', 'ctx')
Inputs may be any that keep to these rules, and one draw needn't show every extreme that they name: `group_order`: each row holds every number once.
All inputs are finite; a program needn't handle non-finite values.
Results may differ from a plain program's by a relative error of at most 0.0075.
Values may be sent and summed in bfloat16 or wider, within the bound.
A program may use at most 64 MiB of HBM per device.

v0:
```python
import jax
import jax.numpy as jnp
from jax import lax
from jax.sharding import PartitionSpec as P

GROUP = 32


def shifted(array, axis, by):
    size = lax.axis_size(axis)
    return lax.ppermute(array, axis, [(i, (i + by) % size) for i in range(size)])


def pair_grads(query_blk, grad_blk, lse_blk, delta_blk, query_pos, key_blk, value_blk, key_pos):
    factor = query_blk.shape[2] ** (-0.5)
    scores = (
        jnp.einsum("qhd,khd->hqk", query_blk, key_blk, preferred_element_type=jnp.float32) * factor
    )
    visible = key_pos[None, None, :] <= query_pos[None, :, None]
    probs = jnp.where(visible, jnp.exp(scores - lse_blk[:, :, None]), 0.0)
    probs_low = probs.astype(jnp.bfloat16)
    value_part = jnp.einsum("hqk,qhd->khd", probs_low, grad_blk, preferred_element_type=jnp.float32)
    dprobs = jnp.einsum("qhd,khd->hqk", grad_blk, value_blk, preferred_element_type=jnp.float32)
    dscores = (probs * (dprobs - delta_blk[:, :, None])).astype(jnp.bfloat16)
    query_part = (
        jnp.einsum("hqk,khd->qhd", dscores, key_blk, preferred_element_type=jnp.float32) * factor
    )
    key_part = (
        jnp.einsum("hqk,qhd->khd", dscores, query_blk, preferred_element_type=jnp.float32) * factor
    )
    rows = query_blk.shape[0]
    width = query_blk.shape[1] * query_blk.shape[2]
    return (
        query_part.reshape(rows, width),
        key_part.reshape(key_blk.shape[0], width),
        value_part.reshape(key_blk.shape[0], width),
    )


def on_device(queries, keys, values, out_grad, out_proj, attn_out, log_sum, group_order):
    tokens = queries.shape[1]
    width = queries.shape[2]
    heads = log_sum.shape[1]
    head_size = width // heads
    upstream = out_grad[0]
    attn_full = jnp.dot(
        upstream,
        lax.all_gather(out_proj, "dp", axis=0, tiled=True),
        preferred_element_type=jnp.float32,
    )
    attn_grad = attn_full.astype(jnp.bfloat16)
    grad_blk = attn_grad.reshape(tokens, heads, head_size)
    out_blk = attn_out[0].reshape(tokens, heads, head_size)
    delta = jnp.sum(grad_blk.astype(jnp.float32) * out_blk.astype(jnp.float32), axis=2).T
    lse_own = log_sum[0]
    order = group_order[0]
    per_block = tokens // GROUP
    cycle_size = lax.axis_size("ctx")
    here = lax.axis_index("ctx")

    def positions(device):
        group_ids = lax.dynamic_slice_in_dim(order, device * per_block, per_block)
        offsets = jnp.arange(GROUP, dtype=jnp.int32)
        return (group_ids[:, None] * GROUP + offsets[None, :]).reshape(tokens)

    own_pos = positions(here)
    query_blk = queries[0].reshape(tokens, heads, head_size)
    key_flat = keys[0]
    value_flat = values[0]
    key_blk = key_flat.reshape(tokens, heads, head_size)
    value_blk = value_flat.reshape(tokens, heads, head_size)
    own = pair_grads(query_blk, grad_blk, lse_own, delta, own_pos, key_blk, value_blk, own_pos)
    key_prev, value_prev = shifted((key_flat, value_flat), "ctx", 1)
    prev_pos = positions((here - 1 + cycle_size) % cycle_size)
    cross = pair_grads(
        query_blk,
        grad_blk,
        lse_own,
        delta,
        own_pos,
        key_prev.reshape(tokens, heads, head_size),
        value_prev.reshape(tokens, heads, head_size),
        prev_pos,
    )
    key_back, value_back = shifted((cross[1], cross[2]), "ctx", -1)
    query_total = own[0] + cross[0]
    key_total = own[1] + key_back
    value_total = own[2] + value_back
    return (
        query_total.astype(jnp.bfloat16).reshape(1, tokens, width),
        key_total.astype(jnp.bfloat16).reshape(1, tokens, width),
        value_total.astype(jnp.bfloat16).reshape(1, tokens, width),
    )


def solution(mesh):
    return jax.shard_map(
        on_device,
        mesh=mesh,
        in_specs=(
            P("dp", "ctx", None),
            P("dp", "ctx", None),
            P("dp", "ctx", None),
            P("dp", "ctx", None),
            P("dp", None),
            P("dp", "ctx", None),
            P("dp", None, "ctx"),
            P("dp", None),
        ),
        out_specs=(P("dp", "ctx", None), P("dp", "ctx", None), P("dp", "ctx", None)),
        check_vma=False,
    )
```

profile of v0, /device:TPU:1, one launch (start us, length us, event | category | flops | bytes accessed | tf_op | source)
XLA Modules:
  0.0 186.6 jit_solution(16854233429764616080)
XLA Ops:
  7.2 0.0 copy-start
  7.2 0.0 copy-start.5
  7.2 0.0 all-gather.2.cloned.1.call-start
  7.2 0.7 all-gather.2.cloned.1.call-update
  7.9 2.0 %copy.64 = bf16[1,128,2048]{1,2,0:T(8,128)(2,1)} copy(bf16[1,128,2048]{2,1,0:T(8,128)(2,1)} %param.10) | data formatting | bytes 1048576 | tf_op args[2]
  10.0 4.4 %collective-permute-start.1 = (bf16[128,2048]{0,1:T(8,128)(2,1)}, bf16[128,2048]{0,1:T(8,128)(2,1)}, u32[]{:S(2)}, u32[]{:S(2)}) collective-permute-start(bf16[128,2048]{0,1:T(8,128)(2,1)} %bitcast.7), channel_id=1, source_target_pairs={{0,1},{1,2},{2,3},{3,4},{4,5},{5,6},{6,7},{7,8},{8,9},{9,10},{10,1... | collective-permute-start | bytes 1572872 | tf_op jit(solution)/shard_map/ppermute | solution.py:11
  14.3 1.3 copy.89
  15.6 0.0 copy-start.2
  15.7 3.5 %collective-permute-start = (bf16[128,2048]{0,1:T(8,128)(2,1)S(1)}, bf16[128,2048]{0,1:T(8,128)(2,1)S(1)}, u32[]{:S(2)}, u32[]{:S(2)}) collective-permute-start(bf16[128,2048]{0,1:T(8,128)(2,1)S(1)} %bitcast.70), channel_id=1, source_target_pairs={{0,1},{1,2},{2,3},{3,4},{4,5},{5,6},{6,7},{7,8},{8,9},{9,10},{10,1... | collective-permute-start | bytes 1572872 | tf_op jit(solution)/shard_map/ppermute | solution.py:11
  19.2 0.8 multiply_bitcast_fusion
  20.0 1.1 convert_bitcast_fusion
  21.2 0.1 iota_add_fusion
  21.3 0.1 add.89
  21.3 0.1 add.82
  21.4 1.3 copy.88
  22.7 2.0 %copy.91 = bf16[16,8,16,128]{3,2,1,0:T(8,128)(2,1)} copy(bf16[16,8,16,128]{3,1,2,0:T(8,128)(2,1)} %bitcast.78) | data formatting | bytes 1048576
  24.7 1.3 copy.92
  26.0 0.1 broadcast_compare_fusion
  26.0 0.0 copy-done.5
  26.1 0.5 fusion.10
  26.6 19.5 %collective-permute-done = bf16[128,2048]{0,1:T(8,128)(2,1)S(1)} collective-permute-done((bf16[128,2048]{0,1:T(8,128)(2,1)S(1)}, bf16[128,2048]{0,1:T(8,128)(2,1)S(1)}, u32[]{:S(2)}, u32[]{:S(2)}) %collective-permute-start) | collective-permute-done | bytes 524320 | tf_op jit(solution)/shard_map/ppermute | solution.py:11
  46.1 0.0 copy-start.4
  46.1 1.5 fusion.6
  47.6 57.5 %all-gather.2.cloned.1.call-done = bf16[2048,2048]{1,0:T(8,128)(2,1)} async-done(((bf16[128,2048]{1,0:T(8,128)(2,1)}), bf16[2048,2048]{1,0:T(8,128)(2,1)}) %all-gather.2.cloned.1.call-update) | async-done | bytes 8388624 | tf_op jit(solution)/shard_map/all_gather | solution.py:48
  105.2 0.0 copy-done.4
  105.2 0.0 copy-done
  105.2 4.6 %fusion.15 = bf16[16,8,16,128]{3,1,2,0:T(8,128)(2,1)S(1)} fusion(bf16[2048,2048]{1,0:T(8,128)(2,1)} %all-gather.2.cloned.1.call-done, bf16[1,128,2048]{2,1,0:T(8,128)(2,1)S(1)} %copy-done), kind=kOutput, calls=%fused_computation.23 | convolution fusion | flops 1074003968 | bytes 9437184 | tf_op jit(solution)/shard_map/dot_general | solution.py:46
  109.8 0.0 copy-done.2
  109.8 0.1 copy.90
  109.9 0.5 copy.76
  110.4 1.3 fusion.22
  111.7 2.5 %copy.79 = f32[128,2048]{1,0:T(8,128)} copy(f32[128,2048]{0,1:T(8,128)} %bitcast.74) | data formatting | bytes 2097152 | tf_op jit(solution)/shard_map/reshape | solution.py:36
  114.2 2.5 %fusion.20 = f32[16,128,128]{2,1,0:T(8,128)} fusion(bf16[128,16,128]{0,2,1:T(8,128)(2,1)S(1)} %copy.76, f32[16,128,128]{2,1,0:T(8,128)} %fusion.6), kind=kOutput, calls=%fused_computation.32 | convolution fusion | flops 67371008 | bytes 2621440 | tf_op jit(solution)/shard_map/hqk,qhd->khd/dot_general | solution.py:22
  116.7 2.6 %copy.78 = f32[128,2048]{1,0:T(8,128)} copy(f32[128,2048]{0,1:T(8,128)} %bitcast.75) | data formatting | bytes 2097152 | tf_op jit(solution)/shard_map/reshape | solution.py:36
  119.3 1.6 multiply_reduce_fusion
  120.9 0.1 copy.59
  120.9 0.0 collective-permute-done.1
  120.9 1.9 %fusion.12 = bf16[16,128,128]{2,1,0:T(8,128)(2,1)S(1)} fusion(f32[16,128,128]{2,1,0:T(8,128)} %fusion.6, bf16[128,16,128]{0,2,1:T(8,128)(2,1)S(1)} %copy.76, bf16[128,16,128]{0,2,1:T(8,128)(2,1)} %bitcast.8, f32[16,128]{1,0:T(8,128)S(1)} %copy.59), kind=kOutput, calls=%fused_computation.20 | convolution fusion | flops 67895296 | bytes 2629632 | tf_op jit(solution)/shard_map/qhd,khd->hqk/dot_general | solution.py:23
  122.9 1.5 fusion
  124.4 2.6 %copy.75 = f32[128,16,128]{0,2,1:T(8,128)} copy(f32[128,16,128]{2,0,1:T(8,128)} %fusion) | data formatting | bytes 2097152 | tf_op jit(solution)/shard_map/mul | solution.py:29
  126.9 5.7 %collective-permute-start.2 = (f32[128,2048]{0,1:T(8,128)}, f32[128,2048]{0,1:T(8,128)}, u32[]{:S(2)}, u32[]{:S(2)}) collective-permute-start(f32[128,2048]{0,1:T(8,128)} %bitcast.82), channel_id=1, source_target_pairs={{0,31},{1,0},{2,1},{3,2},{4,3},{5,4},{6,5},{7,6},{8,7},{9,8},{10,9... | collective-permute-start | bytes 3145736 | tf_op jit(solution)/shard_map/ppermute | solution.py:11
  132.6 3.0 %collective-permute-start.3 = (f32[128,2048]{1,0:T(8,128)}, f32[128,2048]{1,0:T(8,128)}, u32[]{:S(2)}, u32[]{:S(2)}) collective-permute-start(f32[128,2048]{1,0:T(8,128)} %copy.78), channel_id=1, source_target_pairs={{0,31},{1,0},{2,1},{3,2},{4,3},{5,4},{6,5},{7,6},{8,7},{9,8},{10,9... | collective-permute-start | bytes 3145736 | tf_op jit(solution)/shard_map/ppermute | solution.py:11
  135.6 1.6 fusion.11
  137.3 0.0 copy-start.1
  137.3 0.8 copy-done.1
  138.1 0.0 copy-start.3
  138.1 1.6 fusion.24
  139.7 1.5 fusion.14
  141.2 0.3 copy.69
  141.5 1.0 copy.80
  142.5 2.6 %fusion.1 = f32[128,16,128]{2,0,1:T(8,128)} fusion(bf16[16,128,128]{2,1,0:T(8,128)(2,1)} %copy-done.1, bf16[128,16,128]{0,2,1:T(8,128)(2,1)S(1)} %bitcast.67), kind=kOutput, calls=%fused_computation.4 | convolution fusion | flops 67371008 | bytes 2097152 | tf_op jit(solution)/shard_map/hqk,qhd->khd/dot_general | solution.py:29
  145.1 1.6 copy.72
  146.6 8.5 %collective-permute-done.2 = f32[128,2048]{0,1:T(8,128)} collective-permute-done((f32[128,2048]{0,1:T(8,128)}, f32[128,2048]{0,1:T(8,128)}, u32[]{:S(2)}, u32[]{:S(2)}) %collective-permute-start.2) | collective-permute-done | bytes 1048608 | tf_op jit(solution)/shard_map/ppermute | solution.py:11
  155.2 1.3 fusion.16
  156.5 1.0 copy.81
  157.5 20.1 %collective-permute-done.3 = f32[128,2048]{1,0:T(8,128)} collective-permute-done((f32[128,2048]{1,0:T(8,128)}, f32[128,2048]{1,0:T(8,128)}, u32[]{:S(2)}, u32[]{:S(2)}) %collective-permute-start.3) | collective-permute-done | bytes 1048608 | tf_op jit(solution)/shard_map/ppermute | solution.py:11
  177.6 0.0 copy-done.3
  177.6 2.1 %fusion.17 = bf16[1,128,2048]{2,1,0:T(8,128)(2,1)} fusion(f32[128,2048]{1,0:T(8,128)S(1)} %copy-done.3, f32[128,2048]{1,0:T(8,128)} %collective-permute-done.3), kind=kLoop, calls=%fused_computation.29 | loop fusion | flops 524288 | bytes 2621440 | tf_op jit(solution)/shard_map/reshape | solution.py:92
Async XLA Ops:
  7.2 98.0 %copy-start = (bf16[1,128,2048]{2,1,0:T(8,128)(2,1)S(1)}, bf16[1,128,2048]{2,1,0:T(8,128)(2,1)}, u32[]{:S(2)}) copy-start(bf16[1,128,2048]{2,1,0:T(8,128)(2,1)} %param.11) | copy-start | bytes 1572868
  7.2 18.9 %copy-start.5 = (f32[1,16,128]{2,1,0:T(8,128)S(1)}, f32[1,16,128]{2,1,0:T(8,128)}, u32[]{:S(2)}) copy-start(f32[1,16,128]{2,1,0:T(8,128)} %param.14) | copy-start | bytes 24580
  7.2 98.0 %all-gather.2.cloned.1.call-start = ((), (), s32[]{:S(2)}) async-start(), calls=%async_computation | async-start | bytes 8912896 | tf_op jit(solution)/shard_map/all_gather | solution.py:48
  10.0 111.0 %collective-permute-start.1 = (bf16[128,2048]{0,1:T(8,128)(2,1)}, bf16[128,2048]{0,1:T(8,128)(2,1)}, u32[]{:S(2)}, u32[]{:S(2)}) collective-permute-start(bf16[128,2048]{0,1:T(8,128)(2,1)} %bitcast.7), channel_id=1, source_target_pairs={{0,1},{1,2},{2,3},{3,4},{4,5},{5,6},{6,7},{7,8},{8,9},{9,10},{10,1... | collective-permute-start | bytes 1572872 | tf_op jit(solution)/shard_map/ppermute | solution.py:11
  15.6 94.2 %copy-start.2 = (bf16[1,128,2048]{1,2,0:T(8,128)(2,1)}, bf16[1,128,2048]{1,2,0:T(8,128)(2,1)S(1)}, u32[]{:S(2)}) copy-start(bf16[1,128,2048]{1,2,0:T(8,128)(2,1)S(1)} %copy.89) | copy-start | bytes 1572868
  15.7 30.5 %collective-permute-start = (bf16[128,2048]{0,1:T(8,128)(2,1)S(1)}, bf16[128,2048]{0,1:T(8,128)(2,1)S(1)}, u32[]{:S(2)}, u32[]{:S(2)}) collective-permute-start(bf16[128,2048]{0,1:T(8,128)(2,1)S(1)} %bitcast.70), channel_id=1, source_target_pairs={{0,1},{1,2},{2,3},{3,4},{4,5},{5,6},{6,7},{7,8},{8,9},{9,10},{10,1... | collective-permute-start | bytes 1572872 | tf_op jit(solution)/shard_map/ppermute | solution.py:11
  46.1 59.0 %copy-start.4 = (bf16[128,2048]{0,1:T(8,128)(2,1)}, bf16[128,2048]{0,1:T(8,128)(2,1)S(1)}, u32[]{:S(2)}) copy-start(bf16[128,2048]{0,1:T(8,128)(2,1)S(1)} %collective-permute-done) | copy-start | bytes 1572868
  126.9 28.2 %collective-permute-start.2 = (f32[128,2048]{0,1:T(8,128)}, f32[128,2048]{0,1:T(8,128)}, u32[]{:S(2)}, u32[]{:S(2)}) collective-permute-start(f32[128,2048]{0,1:T(8,128)} %bitcast.82), channel_id=1, source_target_pairs={{0,31},{1,0},{2,1},{3,2},{4,3},{5,4},{6,5},{7,6},{8,7},{9,8},{10,9... | collective-permute-start | bytes 3145736 | tf_op jit(solution)/shard_map/ppermute | solution.py:11
  132.6 45.0 %collective-permute-start.3 = (f32[128,2048]{1,0:T(8,128)}, f32[128,2048]{1,0:T(8,128)}, u32[]{:S(2)}, u32[]{:S(2)}) collective-permute-start(f32[128,2048]{1,0:T(8,128)} %copy.78), channel_id=1, source_target_pairs={{0,31},{1,0},{2,1},{3,2},{4,3},{5,4},{6,5},{7,6},{8,7},{9,8},{10,9... | collective-permute-start | bytes 3145736 | tf_op jit(solution)/shard_map/ppermute | solution.py:11
  137.3 0.8 copy-start.1
  138.1 39.6 %copy-start.3 = (f32[128,2048]{1,0:T(8,128)S(1)}, f32[128,2048]{1,0:T(8,128)}, u32[]{:S(2)}) copy-start(f32[128,2048]{1,0:T(8,128)} %copy.79) | copy-start | bytes 3145732
Sparse Core Ops, SparseCore 0:
  11.3 93.8 all-gather.1
where the time goes:
time: 188 us; the launch traced here: 187 us
  waiting for transfers between devices  106 us (56%)
  matrix products  21.2 us (11%)
  local copies, waits for them, and re-layouts  21 us (11%)
  starting transfers between devices  16.6 us (9%)
  between operations  14.2 us (8%)
  other arithmetic  7.12 us (4%)
    all_gather x1, waiting for transfers between devices, on_device(): lax.all_gather(out_proj, 'dp', axis=0, tiled=True)  57.5 us
    ppermute x4, waiting for transfers between devices, shifted(): lax.ppermute(array, axis, [(i, (i + by) % size) for i in range(size)])  48.2 us
    ppermute x4, starting transfers between devices, shifted(): lax.ppermute(array, axis, [(i, (i + by) % size) for i in range(size)])  16.6 us
    unnamed x18, local copies, waits for them, and re-layouts  8.2 us
    reshape x2, local copies, waits for them, and re-layouts, pair_grads(): value_part.reshape(key_blk.shape[0], width)  5.09 us
    dot_general x1, matrix products, on_device(): jnp.dot(upstream, lax.all_gather(out_proj, 'dp', axis=0, tiled=True), pre...  4.65 us
    mul x2, local copies, waits for them, and re-layouts, pair_grads(): jnp.einsum('hqk,qhd->khd', dscores, query_blk, preferred_element_type=jnp...  4.11 us
    dot_general x2, matrix products, pair_grads(): jnp.einsum('hqk,qhd->khd', dscores, query_blk, preferred_element_type=jnp...  4.05 us
  transfers between devices with their start and end apart: 5, of which 4 were waited for; matrix products, arithmetic and copies ran while one was open for 22% of the time, Pallas kernels for 0%

commit v1 on v0

--- a/solution.py
+++ b/solution.py
@@ -2,6 +2,7 @@
 import jax.numpy as jnp
 from jax import lax
 from jax.sharding import PartitionSpec as P
+from jax.lax import all_to_all, axis_size
 
 GROUP = 32
 
@@ -38,15 +39,19 @@
 
 
 def on_device(queries, keys, values, out_grad, out_proj, attn_out, log_sum, group_order):
+
+    def perform_routes_all_over_axis(inputs):
+        return jnp.concatenate(
+            all_to_all(jnp.stack([inputs for _ in range(axis_size("dp"))]), "dp", 0, 0), axis=0
+        )
+
     tokens = queries.shape[1]
     width = queries.shape[2]
     heads = log_sum.shape[1]
     head_size = width // heads
     upstream = out_grad[0]
     attn_full = jnp.dot(
-        upstream,
-        lax.all_gather(out_proj, "dp", axis=0, tiled=True),
-        preferred_element_type=jnp.float32,
+        upstream, perform_routes_all_over_axis(out_proj), preferred_element_type=jnp.float32
     )
     attn_grad = attn_full.astype(jnp.bfloat16)
     grad_blk = attn_grad.reshape(tokens, heads, head_size)

time: 188 us -> 224 us (1.19)
  waiting for transfers between devices: 106 us -> 143 us
  between operations: 14.2 us -> 0.85 us
  starting transfers between devices: 16.6 us -> 23.7 us
  matrix products: 21.2 us -> 24.6 us
  local copies, waits for them, and re-layouts: 21 us -> 23.4 us
    all_to_all x0 -> x1, waiting for transfers between devices: none -> 103 us  [perform_routes_all_over_axis(): all_to_all(jnp.stack([inputs for _ in range(axis_size('dp'))]), 'dp', 0, 0)]
    all_gather x1 -> x0, waiting for transfers between devices: 57.5 us -> none  [on_device(): lax.all_gather(out_proj, 'dp', axis=0, tiled=True)]
    all_to_all x0 -> x1, starting transfers between devices: none -> 11.4 us  [perform_routes_all_over_axis(): all_to_all(jnp.stack([inputs for _ in range(axis_size('dp'))]), 'dp', 0, 0)]
    ppermute x4, waiting for transfers between devices: 48.2 us -> 40.5 us  [shifted(): lax.ppermute(array, axis, [(i, (i + by) % size) for i in range(size)])]
    another operation x0 -> x1, local copies, waits for them, and re-layouts: none -> 5.41 us  [perform_routes_all_over_axis(): jnp.stack([inputs for _ in range(axis_size('dp'))])]
    ppermute x4, starting transfers between devices: 16.6 us -> 12.3 us  [shifted(): lax.ppermute(array, axis, [(i, (i + by) % size) for i in range(size)])]
    unnamed x18 -> x22, local copies, waits for them, and re-layouts: 8.2 us -> 5.27 us
  transfers between devices with their start and end apart: 5 -> 5, of which waited for: 4 -> 4; matrix products, arithmetic and copies ran while one was open for 22% -> 18% of each run, Pallas kernels for 0% -> 0%
where the time goes in v1:
time: 224 us; the launch traced here: 221 us
  waiting for transfers between devices  143 us (64%)
  matrix products  24.6 us (11%)
  starting transfers between devices  23.7 us (11%)
  local copies, waits for them, and re-layouts  23.4 us (10%)
  other arithmetic  5.68 us (3%)
    all_to_all x1, waiting for transfers between devices, perform_routes_all_over_axis(): all_to_all(jnp.stack([inputs for _ in range(axis_size('dp'))]), 'dp', 0, 0)  103 us
    ppermute x4, waiting for transfers between devices, shifted(): lax.ppermute(array, axis, [(i, (i + by) % size) for i in range(size)])  40.5 us
    ppermute x4, starting transfers between devices, shifted(): lax.ppermute(array, axis, [(i, (i + by) % size) for i in range(size)])  12.3 us
    all_to_all x1, starting transfers between devices, perform_routes_all_over_axis(): all_to_all(jnp.stack([inputs for _ in range(axis_size('dp'))]), 'dp', 0, 0)  11.4 us
    another operation x1, local copies, waits for them, and re-layouts, perform_routes_all_over_axis(): jnp.stack([inputs for _ in range(axis_size('dp'))])  5.41 us
    dot_general x2, matrix products, pair_grads(): jnp.einsum('hqk,khd->qhd', dscores, key_blk, preferred_element_type=jnp.f...  5.35 us
    unnamed x22, local copies, waits for them, and re-layouts  5.27 us
    mul x2, local copies, waits for them, and re-layouts, pair_grads(): jnp.einsum('hqk,qhd->khd', dscores, query_blk, preferred_element_type=jnp...  5.08 us
  transfers between devices with their start and end apart: 5, of which 4 were waited for; matrix products, arithmetic and copies ran while one was open for 18% of the time, Pallas kernels for 0%

profile of v1, /device:TPU:1, one launch (start us, length us, event | category | flops | bytes accessed | tf_op | source)
XLA Modules:
  0.0 221.5 jit_solution(15571913227536469566)
XLA Ops:
  0.6 0.0 copy-start
  0.6 5.4 %stack.2 = bf16[16,128,2048]{2,1,0:T(8,128)(2,1)} broadcast(bf16[128,2048]{1,0:T(8,128)(2,1)} %param.12), dimensions={1,2} | broadcast | bytes 8912896 | tf_op jit(solution)/shard_map/stack | solution.py:45
  6.1 0.0 copy-start.5
  6.1 0.0 copy-start.3
  6.1 0.0 copy-start.7
  6.1 0.0 copy-start.4
  6.1 0.0 copy-start.6
  6.1 11.4 %all-to-all-start = ((bf16[16,128,2048]{2,1,0:T(8,128)(2,1)}), bf16[16,128,2048]{2,1,0:T(8,128)(2,1)}, u32[]{:S(2)}, u32[]{:S(2)}) async-start(bf16[16,128,2048]{2,1,0:T(8,128)(2,1)} %stack.2), calls=%async_computation | async-start | bytes 16777216 | tf_op jit(solution)/shard_map/all_to_all | solution.py:45
  17.5 0.0 copy-done.5
  17.5 0.3 copy.89
  17.8 0.0 copy-start.2
  17.8 1.9 collective-permute-start
  19.7 0.0 copy-done.3
  19.8 1.0 copy.64
  20.8 2.3 %collective-permute-start.1 = (bf16[128,2048]{0,1:T(8,128)(2,1)}, bf16[128,2048]{0,1:T(8,128)(2,1)}, u32[]{:S(2)}, u32[]{:S(2)}) collective-permute-start(bf16[128,2048]{0,1:T(8,128)(2,1)} %bitcast.8), channel_id=1, source_target_pairs={{0,1},{1,2},{2,3},{3,4},{4,5},{5,6},{6,7},{7,8},{8,9},{9,10},{10,1... | collective-permute-start | bytes 1572872 | tf_op jit(solution)/shard_map/ppermute | solution.py:12
  23.1 0.0 copy-done.7
  23.1 0.1 multiply_bitcast_fusion
  23.2 0.0 copy-done.4
  23.2 0.1 convert_bitcast_fusion
  23.3 0.1 iota_add_fusion
  23.3 1.3 copy.88
  24.7 0.1 add.89
  24.7 0.1 add.82
  24.8 0.9 copy.91
  25.7 1.2 copy.92
  26.9 0.1 broadcast_compare_fusion
  27.0 0.0 copy-done.6
  27.0 0.5 fusion.10
  27.6 19.1 %collective-permute-done = bf16[128,2048]{0,1:T(8,128)(2,1)} collective-permute-done((bf16[128,2048]{0,1:T(8,128)(2,1)S(1)}, bf16[128,2048]{0,1:T(8,128)(2,1)}, u32[]{:S(2)}, u32[]{:S(2)}) %collective-permute-start) | collective-permute-done | bytes 524320 | tf_op jit(solution)/shard_map/ppermute | solution.py:12
  46.7 2.6 %fusion.6 = f32[16,128,128]{2,1,0:T(8,128)} fusion(bf16[128,16,128]{0,2,1:T(8,128)(2,1)S(1)} %bitcast.66, bf16[128,16,128]{0,2,1:T(8,128)(2,1)} %bitcast.7, f32[16,128]{1,0:T(8,128)S(1)} %bitcast.84, pred[128,128]{1,0:T(8,128)(4,1)S(1)} %get-tuple-element.9), kind=kOutput, calls=%fused_computation.12 | convolution fusion | flops 67895296 | bytes 2121728 | tf_op jit(solution)/shard_map/qhd,khd->hqk/dot_general | solution.py:18
  49.3 102.7 %all-to-all-done = bf16[16,128,2048]{2,1,0:T(8,128)(2,1)} async-done(((bf16[16,128,2048]{2,1,0:T(8,128)(2,1)}), bf16[16,128,2048]{2,1,0:T(8,128)(2,1)}, u32[]{:S(2)}, u32[]{:S(2)}) %all-to-all-start) | async-done | bytes 8388640 | tf_op jit(solution)/shard_map/all_to_all | solution.py:45
  152.0 0.0 copy-done
  152.0 4.6 %fusion.15 = bf16[16,8,16,128]{3,1,2,0:T(8,128)(2,1)S(1)} fusion(bf16[2048,2048]{1,0:T(8,128)(2,1)} %bitcast.3, bf16[1,128,2048]{2,1,0:T(8,128)(2,1)S(1)} %copy-done), kind=kOutput, calls=%fused_computation.23 | convolution fusion | flops 1074003968 | bytes 9437184 | tf_op jit(solution)/shard_map/dot_general | solution.py:53
  156.7 0.0 copy-done.2
  156.7 0.1 copy.90
  156.8 0.5 copy.76
  157.3 1.6 multiply_reduce_fusion
  158.8 0.1 copy.59
  158.9 1.6 fusion.11
  160.5 0.0 copy-start.1
  160.5 2.7 %fusion.24 = f32[16,128,128]{2,1,0:T(8,128)} fusion(bf16[16,128,128]{2,1,0:T(8,128)(2,1)S(1)} %fusion.11, bf16[128,16,128]{0,2,1:T(8,128)(2,1)} %bitcast.73), kind=kOutput, calls=%fused_computation.42 | convolution fusion | flops 67108864 | bytes 2097152 | tf_op jit(solution)/shard_map/hqk,khd->qhd/dot_general | solution.py:27
  163.2 0.0 collective-permute-done.1
  163.2 0.0 copy-done.1
  163.2 1.9 fusion.12
  165.2 1.5 fusion
  166.7 2.5 %copy.75 = f32[128,16,128]{0,2,1:T(8,128)} copy(f32[128,16,128]{2,0,1:T(8,128)} %fusion) | data formatting | bytes 2097152 | tf_op jit(solution)/shard_map/mul | solution.py:30
  169.2 5.4 %collective-permute-start.2 = (f32[128,2048]{0,1:T(8,128)}, f32[128,2048]{0,1:T(8,128)}, u32[]{:S(2)}, u32[]{:S(2)}) collective-permute-start(f32[128,2048]{0,1:T(8,128)} %bitcast.81), channel_id=1, source_target_pairs={{0,31},{1,0},{2,1},{3,2},{4,3},{5,4},{6,5},{7,6},{8,7},{9,8},{10,9... | collective-permute-start | bytes 3145736 | tf_op jit(solution)/shard_map/ppermute | solution.py:12
  174.7 2.7 %fusion.14 = bf16[128,16,128]{2,0,1:T(8,128)(2,1)} fusion(f32[16,128,128]{2,1,0:T(8,128)} %fusion.24, bf16[16,128,128]{2,1,0:T(8,128)(2,1)S(1)} %fusion.12, bf16[128,16,128]{0,2,1:T(8,128)(2,1)} %bitcast.7), kind=kOutput, calls=%fused_computation.22 | convolution fusion | flops 67895296 | bytes 2621440 | tf_op jit(solution)/shard_map/hqk,khd->qhd/dot_general | solution.py:27
  177.3 1.3 copy.69
  178.6 1.0 copy.80
  179.6 2.5 %fusion.20 = f32[16,128,128]{2,1,0:T(8,128)} fusion(bf16[128,16,128]{0,2,1:T(8,128)(2,1)S(1)} %copy.76, f32[16,128,128]{2,1,0:T(8,128)} %fusion.6), kind=kOutput, calls=%fused_computation.32 | convolution fusion | flops 67371008 | bytes 2621440 | tf_op jit(solution)/shard_map/hqk,qhd->khd/dot_general | solution.py:23
  182.1 2.5 %copy.78 = f32[128,2048]{1,0:T(8,128)} copy(f32[128,2048]{0,1:T(8,128)} %bitcast.76) | data formatting | bytes 2097152 | tf_op jit(solution)/shard_map/reshape | solution.py:37
  184.7 2.6 %collective-permute-start.3 = (f32[128,2048]{1,0:T(8,128)}, f32[128,2048]{1,0:T(8,128)}, u32[]{:S(2)}, u32[]{:S(2)}) collective-permute-start(f32[128,2048]{1,0:T(8,128)} %copy.78), channel_id=1, source_target_pairs={{0,31},{1,0},{2,1},{3,2},{4,3},{5,4},{6,5},{7,6},{8,7},{9,8},{10,9... | collective-permute-start | bytes 3145736 | tf_op jit(solution)/shard_map/ppermute | solution.py:12
  187.3 2.6 %fusion.1 = f32[128,16,128]{2,0,1:T(8,128)} fusion(bf16[16,128,128]{2,1,0:T(8,128)(2,1)} %copy-done.1, bf16[128,16,128]{0,2,1:T(8,128)(2,1)S(1)} %bitcast.68), kind=kOutput, calls=%fused_computation.4 | convolution fusion | flops 67371008 | bytes 2097152 | tf_op jit(solution)/shard_map/hqk,qhd->khd/dot_general | solution.py:30
  189.9 2.5 %copy.72 = f32[128,16,128]{0,2,1:T(8,128)} copy(f32[128,16,128]{2,0,1:T(8,128)} %fusion.1) | data formatting | bytes 2097152 | tf_op jit(solution)/shard_map/mul | solution.py:30
  192.4 1.3 fusion.22
  193.7 1.6 copy.79
  195.3 1.6 collective-permute-done.2
  196.9 1.6 fusion.16
  198.5 1.0 copy.81
  199.5 19.8 %collective-permute-done.3 = f32[128,2048]{1,0:T(8,128)} collective-permute-done((f32[128,2048]{1,0:T(8,128)}, f32[128,2048]{1,0:T(8,128)}, u32[]{:S(2)}, u32[]{:S(2)}) %collective-permute-start.3) | collective-permute-done | bytes 1048608 | tf_op jit(solution)/shard_map/ppermute | solution.py:12
  219.3 2.1 fusion.17
Async XLA Ops:
  0.6 151.4 %copy-start = (bf16[1,128,2048]{2,1,0:T(8,128)(2,1)S(1)}, bf16[1,128,2048]{2,1,0:T(8,128)(2,1)}, u32[]{:S(2)}) copy-start(bf16[1,128,2048]{2,1,0:T(8,128)(2,1)} %param.11) | copy-start | bytes 1572868
  6.1 11.5 %copy-start.5 = (bf16[1,128,2048]{2,1,0:T(8,128)(2,1)S(1)}, bf16[1,128,2048]{2,1,0:T(8,128)(2,1)}, u32[]{:S(2)}) copy-start(bf16[1,128,2048]{2,1,0:T(8,128)(2,1)} %param.9) | copy-start | bytes 1572868
  6.1 13.7 %copy-start.3 = (bf16[1,128,2048]{2,1,0:T(8,128)(2,1)S(1)}, bf16[1,128,2048]{2,1,0:T(8,128)(2,1)}, u32[]{:S(2)}) copy-start(bf16[1,128,2048]{2,1,0:T(8,128)(2,1)} %param.10) | copy-start | bytes 1572868
  6.1 17.0 %copy-start.7 = (s32[1,128]{1,0:T(1,128)S(1)}, s32[1,128]{1,0:T(1,128)}, u32[]{:S(2)}) copy-start(s32[1,128]{1,0:T(1,128)} %param.15) | copy-start | bytes 1540
  6.1 17.1 %copy-start.4 = (bf16[1,128,2048]{2,1,0:T(8,128)(2,1)S(1)}, bf16[1,128,2048]{2,1,0:T(8,128)(2,1)}, u32[]{:S(2)}) copy-start(bf16[1,128,2048]{2,1,0:T(8,128)(2,1)} %param.13) | copy-start | bytes 1572868
  6.1 21.0 %copy-start.6 = (f32[1,16,128]{2,1,0:T(8,128)S(1)}, f32[1,16,128]{2,1,0:T(8,128)}, u32[]{:S(2)}) copy-start(f32[1,16,128]{2,1,0:T(8,128)} %param.14) | copy-start | bytes 24580
  6.1 145.9 %all-to-all-start = ((bf16[16,128,2048]{2,1,0:T(8,128)(2,1)}), bf16[16,128,2048]{2,1,0:T(8,128)(2,1)}, u32[]{:S(2)}, u32[]{:S(2)}) async-start(bf16[16,128,2048]{2,1,0:T(8,128)(2,1)} %stack.2), calls=%async_computation | async-start | bytes 16777216 | tf_op jit(solution)/shard_map/all_to_all | solution.py:45
  17.8 138.8 %copy-start.2 = (bf16[1,128,2048]{1,2,0:T(8,128)(2,1)}, bf16[1,128,2048]{1,2,0:T(8,128)(2,1)S(1)}, u32[]{:S(2)}) copy-start(bf16[1,128,2048]{1,2,0:T(8,128)(2,1)S(1)} %copy.89) | copy-start | bytes 1572868
  17.8 28.9 %collective-permute-start = (bf16[128,2048]{0,1:T(8,128)(2,1)S(1)}, bf16[128,2048]{0,1:T(8,128)(2,1)}, u32[]{:S(2)}, u32[]{:S(2)}) collective-permute-start(bf16[128,2048]{0,1:T(8,128)(2,1)S(1)} %bitcast.71), channel_id=1, source_target_pairs={{0,1},{1,2},{2,3},{3,4},{4,5},{5,6},{6,7},{7,8},{8,9},{9,10},{10,1... | collective-permute-start | bytes 1572872 | tf_op jit(solution)/shard_map/ppermute | solution.py:12
  20.8 142.5 %collective-permute-start.1 = (bf16[128,2048]{0,1:T(8,128)(2,1)}, bf16[128,2048]{0,1:T(8,128)(2,1)}, u32[]{:S(2)}, u32[]{:S(2)}) collective-permute-start(bf16[128,2048]{0,1:T(8,128)(2,1)} %bitcast.8), channel_id=1, source_target_pairs={{0,1},{1,2},{2,3},{3,4},{4,5},{5,6},{6,7},{7,8},{8,9},{9,10},{10,1... | collective-permute-start | bytes 1572872 | tf_op jit(solution)/shard_map/ppermute | solution.py:12
  160.5 2.7 %copy-start.1 = (bf16[16,128,128]{2,1,0:T(8,128)(2,1)}, bf16[16,128,128]{2,1,0:T(8,128)(2,1)S(1)}, u32[]{:S(2)}) copy-start(bf16[16,128,128]{2,1,0:T(8,128)(2,1)S(1)} %fusion.11) | copy-start | bytes 1572868
  169.2 27.7 %collective-permute-start.2 = (f32[128,2048]{0,1:T(8,128)}, f32[128,2048]{0,1:T(8,128)}, u32[]{:S(2)}, u32[]{:S(2)}) collective-permute-start(f32[128,2048]{0,1:T(8,128)} %bitcast.81), channel_id=1, source_target_pairs={{0,31},{1,0},{2,1},{3,2},{4,3},{5,4},{6,5},{7,6},{8,7},{9,8},{10,9... | collective-permute-start | bytes 3145736 | tf_op jit(solution)/shard_map/ppermute | solution.py:12
  184.7 34.7 %collective-permute-start.3 = (f32[128,2048]{1,0:T(8,128)}, f32[128,2048]{1,0:T(8,128)}, u32[]{:S(2)}, u32[]{:S(2)}) collective-permute-start(f32[128,2048]{1,0:T(8,128)} %copy.78), channel_id=1, source_target_pairs={{0,31},{1,0},{2,1},{3,2},{4,3},{5,4},{6,5},{7,6},{8,7},{9,8},{10,9... | collective-permute-start | bytes 3145736 | tf_op jit(solution)/shard_map/ppermute | solution.py:12
